TPU v7x, 256 devices: a whole 4x4x8 slice. The times are simulated.
256 devices in a mesh: rows: 32 (over z, x), far: 8 (over y, core).
Axes of the slice: x: 4, y: 4, z: 8, core: 2. Of those that a mesh axis runs over, the one named last changes fastest.
Arguments:
- right_side: float32 [65536, 256], P('rows'), may hold values from -24 to 24
- near_blocks: float32 [512, 48, 128, 128], P('rows', 'far'), may hold values from -0.0234375 to 0.0234375
- near_cols: int32 [512, 48], P('rows', 'far'), may hold values from 0 to 511, as said below
- far_src: int32 [32, 32, 8], P('rows', None, 'far'), may hold values from 0 to 15
- far_tgt: int32 [32, 32, 8], P('rows', None, 'far'), may hold values from 0 to 15
- far_left: float32 [32, 32, 8, 128, 64], P('rows', None, 'far'), may hold values from -0.0546875 to 0.0546875
- far_right: float32 [32, 32, 8, 128, 64], P('rows', None, 'far'), may hold values from -0.5 to 0.5
Outputs:
- solution: float32 [65536, 256], P('rows', 'far')
- residual: float32 [65536, 256], P('rows', 'far')
Inputs may be any that keep to these rules, and one draw needn't show every extreme that they name: `near_cols`: each near-field column lies within 8 clusters of its row; slot 0 of row i names i itself, slot 1 names min(i + 8, 511) and slot 2 names max(i - 8, 0).
All inputs are finite; a program needn't handle non-finite values.
Results may differ from a plain program's by a relative error of at most 0.0003.
Values sent between devices are 32-bit elements; how exact they have to be, the bound alone decides.
A program may use at most 128 MiB of HBM per device.

v0:
```python
import jax
import jax.numpy as jnp
from jax import lax
from jax.sharding import PartitionSpec as P

B = 128
CL_DEV = 16
REACH = 8
TOP_PRECISION = lax.Precision.HIGHEST
EPS = 1e-06


def with_halo(cells, sides, width):
    for axis, dim in sides:
        count = lax.axis_size(axis)
        ends = count - 1
        head = lax.slice_in_dim(cells, 0, width, axis=dim)
        tail = lax.slice_in_dim(cells, cells.shape[dim] - width, cells.shape[dim], axis=dim)
        cells = jnp.concatenate(
            [
                lax.ppermute(tail, axis, [(i, (i + 1) % count) for i in range(ends)]),
                cells,
                lax.ppermute(head, axis, [((i + 1) % count, i) for i in range(ends)]),
            ],
            axis=dim,
        )
    return cells


def column_dots(left_vec, right_vector):
    return jnp.sum(left_vec * right_vector, axis=0)


def near_term(vector_in, near_blocks, near_cols):
    rhs_count = vector_in.shape[1]
    padded = with_halo(vector_in, (("rows", 0),), REACH * B)
    clusters = padded.reshape(-1, B, rhs_count)
    offset = lax.axis_index("rows") * CL_DEV - REACH
    picked = jnp.take(clusters, near_cols - offset, axis=0)
    return jnp.einsum("cspq,csqn->cpn", near_blocks, picked, precision=TOP_PRECISION)


def far_term(vector_in, far_src, far_tgt, far_left, far_right):
    clusters = vector_in.reshape(CL_DEV, B, vector_in.shape[1])
    picked = jnp.take(clusters, far_src[0], axis=0)
    coefficients = jnp.einsum("tsbr,tsbn->tsrn", far_right[0], picked, precision=TOP_PRECISION)
    owning_devices = (far_tgt[0][:, :, None] == jnp.arange(CL_DEV, dtype=jnp.int32)).astype(
        jnp.float32
    )
    contribution_part = jnp.einsum(
        "asbr,asrn->asbn",
        far_left[0],
        lax.all_to_all(coefficients, "rows", split_axis=0, concat_axis=0, tiled=True),
        precision=TOP_PRECISION,
    )
    return jnp.einsum("hyo,hyze->oze", owning_devices, contribution_part, precision=TOP_PRECISION)


def own_columns(vector_in):
    share_width = vector_in.shape[-1] // lax.axis_size("far")
    return lax.dynamic_slice_in_dim(
        vector_in, lax.axis_index("far") * share_width, share_width, vector_in.ndim - 1
    )


def least_squares(rhs_length, upper_left, lower_left, column_two, lower_right):
    radius_one = jnp.sqrt(upper_left * upper_left + lower_left * lower_left)
    cosine_one = upper_left / radius_one
    sine_one = lower_left / radius_one
    rotated_top = cosine_one * rhs_length
    rotated_mid = -sine_one * rhs_length
    coupled = cosine_one * column_two[0] + sine_one * column_two[1]
    diagonal_two = cosine_one * column_two[1] - sine_one * column_two[0]
    radius_two = jnp.sqrt(diagonal_two * diagonal_two + lower_right * lower_right)
    weight_two = diagonal_two * rotated_mid / (radius_two * radius_two)
    weight_one = (rotated_top - coupled * weight_two) / radius_one
    return (weight_one, weight_two)


def shards(right_side, near_blocks, near_cols, far_src, far_tgt, far_left, far_right):

    def partial_image(vector_in):
        near_part = near_term(vector_in, near_blocks, near_cols)
        far_part = far_term(vector_in, far_src, far_tgt, far_left, far_right)
        return (near_part + far_part).reshape(vector_in.shape)

    def finish(vector_in):
        return own_columns(vector_in)

    def apply_op(vector_in):
        return 0.5 * vector_in + lax.psum(partial_image(vector_in), "far")

    def orthogonal(vectors, candidate):
        heights = lax.psum(jnp.stack([column_dots(item, candidate) for item in vectors]), "rows")
        for slot_id in range(len(vectors)):
            candidate = candidate - heights[slot_id] * vectors[slot_id]
        length = jnp.sqrt(lax.psum(column_dots(candidate, candidate), "rows") + EPS)
        return (heights, candidate, length)

    rhs_length = jnp.sqrt(lax.psum(column_dots(right_side, right_side), "rows") + EPS)
    first_full = right_side / rhs_length
    image_one = apply_op(first_full)
    heights_one, candidate, lower_left = orthogonal((first_full,), image_one)
    second_vec = candidate / lower_left
    image_two = apply_op(second_vec)
    heights_two, candidate, lower_right = orthogonal((first_full, second_vec), image_two)
    weight_one, weight_two = least_squares(
        rhs_length, heights_one[0], lower_left, heights_two, lower_right
    )
    own_solution = weight_one * first_full + weight_two * second_vec
    own_residual = right_side - weight_one * image_one - weight_two * image_two
    return (finish(own_solution), finish(own_residual))


def solution(mesh):
    return jax.shard_map(
        shards,
        mesh=mesh,
        in_specs=(
            P("rows", None),
            P("rows", "far", None, None),
            P("rows", "far"),
            P("rows", None, "far"),
            P("rows", None, "far"),
            P("rows", None, "far", None, None),
            P("rows", None, "far", None, None),
        ),
        out_specs=(P("rows", "far"), P("rows", "far")),
        check_vma=False,
    )
```

profile of v0, /device:TPU:2, one launch (start us, length us, event | category | flops | bytes accessed | tf_op | source)
XLA Modules:
  0.0 811.1 jit_solution(4049094716238253556)
XLA Ops:
  7.2 0.0 copy-start
  7.2 0.8 and_bitcast_fusion
  7.9 0.7 fusion.45
  8.6 1.9 multiply_reduce_fusion.5
  10.5 1.9 copy.35
  12.4 73.7 %psum.49 = f32[256]{0:T(256)S(1)} all-reduce(f32[256]{0:T(256)S(1)} %multiply_reduce_fusion.5), channel_id=1, replica_groups=mesh['rows'=32,'far'=8] {'rows'}, use_global_device_ids=true, to_apply=%region_1.0 | all-reduce | flops 256 | bytes 2048 | tf_op jit(solution)/shard_map/psum | solution.py:100
  86.1 1.6 broadcast_divide_fusion.1
  87.7 2.9 copy.39
  90.7 4.3 gather_fusion.1
  95.0 6.5 fusion.18
  101.5 8.9 %all-to-all-start = ((f32[32,1,64,256]{3,2,1,0:T(8,128)}), f32[32,1,64,256]{3,2,1,0:T(8,128)}, u32[]{:S(2)}, u32[]{:S(2)}) async-start(f32[32,1,64,256]{3,2,1,0:T(8,128)} %fusion.18), calls=%async_computation | async-start | bytes 4194304 | tf_op jit(solution)/shard_map/all_to_all | solution.py:53
  110.3 0.0 copy-start.2
  110.3 0.0 all-reduce.3.cloned.1.call-start
  110.4 3.1 fusion.49
  113.5 3.4 collective-permute-start
  116.9 3.8 collective-permute-start.1
  120.7 0.1 copy.36
  120.8 0.1 copy.38
  120.9 0.1 reshape.164
  121.0 23.6 %collective-permute-done = f32[1024,256]{0,1:T(8,128)} collective-permute-done((f32[1024,256]{0,1:T(8,128)}, f32[1024,256]{0,1:T(8,128)}, u32[]{:S(2)}, u32[]{:S(2)}) %collective-permute-start) | collective-permute-done | bytes 1048608 | tf_op jit(solution)/shard_map/ppermute | solution.py:21
  144.6 2.2 collective-permute-done.1
  146.8 4.5 pad_maximum_fusion
  151.4 5.6 copy.37
  157.0 10.9 %gather_fusion = f32[96,128,256]{2,1,0:T(8,128)} fusion(f32[32,128,256]{2,1,0:T(8,128)} %bitcast.100, s32[1024]{0:T(1024)S(1)} %pad_clamp_fusion.1), kind=kCustom, calls=%fused_computation.clone | custom fusion | bytes 25166208 | tf_op jit(solution)/shard_map/jit(_take)/gather | solution.py:39
  167.9 0.0 all-to-all-done
  167.9 10.1 %convolution_bitcast_fusion.1 = f32[32,128,256]{1,2,0:T(8,128)} fusion(f32[32,1,64,256]{3,2,1,0:T(8,128)} %all-to-all-done, f32[1,32,1,128,64]{3,4,2,1,0:T(8,128)S(1)} %copy-done), kind=kOutput, calls=%fused_computation.21 | convolution fusion | flops 805306368 | bytes 7340032 | tf_op jit(solution)/shard_map/asbr,asrn->asbn/dot_general | solution.py:50
  178.0 5.5 copy.41
  183.5 3.8 fusion.37
  187.3 21.8 %bitcast_add_fusion.1 = f32[16,128,256]{2,1,0:T(8,128)} fusion(f32[16,128,256]{2,0,1:T(8,128)S(1)} %fusion.37, f32[16,6,128,128]{3,2,1,0:T(8,128)} %param.12, f32[16,6,128,256]{3,2,1,0:T(8,128)} %bitcast.102, pred[16,6]{1,0:T(8,128)(4,1)S(1)} %copy.36), kind=kOutput, calls=%fused_computation.23 | convolution fusion | flops 4835508224 | bytes 23068768 | tf_op jit(solution)/shard_map/cspq,csqn->cpn/dot_general | solution.py:40
  209.1 2.9 copy.43
  212.0 0.0 all-reduce.3.cloned.1.call-update
  212.0 89.7 %all-reduce.3.cloned.1.call-done = f32[2048,256]{0,1:T(8,128)} async-done(((f32[2048,256]{0,1:T(8,128)}), f32[2048,256]{0,1:T(8,128)}) %all-reduce.3.cloned.1.call-update) | async-done | bytes 2097168 | tf_op jit(solution)/shard_map/psum | solution.py:91
  301.7 3.3 multiply_add_fusion.1
  305.1 71.1 %psum.51 = f32[256]{0:T(256)S(1)} all-reduce(f32[256]{0:T(256)S(1)} %get-tuple-element.12), channel_id=1, replica_groups=mesh['rows'=32,'far'=8] {'rows'}, use_global_device_ids=true, to_apply=%region_4.7 | all-reduce | flops 256 | bytes 2048 | tf_op jit(solution)/shard_map/psum | solution.py:94
  376.2 2.2 multiply_reduce_fusion.3
  378.4 74.3 %psum.52 = f32[256]{0:T(256)S(1)} all-reduce(f32[256]{0:T(256)S(1)} %multiply_reduce_fusion.3), channel_id=1, replica_groups=mesh['rows'=32,'far'=8] {'rows'}, use_global_device_ids=true, to_apply=%region_6.9 | all-reduce | flops 256 | bytes 2048 | tf_op jit(solution)/shard_map/psum | solution.py:97
  452.7 3.5 broadcast_divide_fusion
  456.2 2.9 copy.47
  459.1 4.3 gather_fusion.3
  463.4 6.5 fusion.21
  469.9 5.9 all-to-all-start.1
  475.8 0.0 all-reduce.5.cloned.1.call-start
  475.9 1.8 fusion.48
  477.7 3.4 collective-permute-start.2
  481.1 2.5 collective-permute-start.3
  483.6 19.2 %collective-permute-done.2 = f32[1024,256]{0,1:T(8,128)S(1)} collective-permute-done((f32[1024,256]{0,1:T(8,128)S(1)}, f32[1024,256]{0,1:T(8,128)S(1)}, u32[]{:S(2)}, u32[]{:S(2)}) %collective-permute-start.2) | collective-permute-done | bytes 1048608 | tf_op jit(solution)/shard_map/ppermute | solution.py:21
  502.8 2.0 collective-permute-done.3
  504.9 2.2 pad_maximum_fusion.1
  507.1 5.8 copy.45
  512.9 10.9 %gather_fusion.2 = f32[96,128,256]{2,1,0:T(8,128)} fusion(f32[32,128,256]{2,1,0:T(8,128)} %bitcast.99, s32[1024]{0:T(1024)S(1)} %pad_clamp_fusion.1), kind=kCustom, calls=%fused_computation.2.clone | custom fusion | bytes 25166208 | tf_op jit(solution)/shard_map/jit(_take)/gather | solution.py:39
  523.8 10.1 %convolution_bitcast_fusion = f32[32,128,256]{1,2,0:T(8,128)} fusion(f32[32,1,64,256]{3,2,1,0:T(8,128)} %all-to-all-done.1, f32[1,32,1,128,64]{3,4,2,1,0:T(8,128)S(1)} %copy-done), kind=kOutput, calls=%fused_computation.20 | convolution fusion | flops 805306368 | bytes 7340032 | tf_op jit(solution)/shard_map/asbr,asrn->asbn/dot_general | solution.py:50
  533.9 5.5 copy.49
  539.4 3.8 fusion.35
  543.2 21.5 %bitcast_add_fusion = f32[16,128,256]{2,1,0:T(8,128)} fusion(f32[16,128,256]{2,0,1:T(8,128)S(1)} %fusion.35, f32[16,6,128,128]{3,2,1,0:T(8,128)} %param.12, f32[16,6,128,256]{3,2,1,0:T(8,128)} %bitcast.101, pred[16,6]{1,0:T(8,128)(4,1)S(1)} %copy.36), kind=kOutput, calls=%fused_computation.22 | convolution fusion | flops 4835508224 | bytes 23068768 | tf_op jit(solution)/shard_map/cspq,csqn->cpn/dot_general | solution.py:40
  564.7 2.9 copy.51
  567.6 0.0 all-reduce.5.cloned.1.call-update
  567.6 82.0 %all-reduce.5.cloned.1.call-done = f32[2048,256]{0,1:T(8,128)} async-done(((f32[2048,256]{0,1:T(8,128)}), f32[2048,256]{0,1:T(8,128)}) %all-reduce.5.cloned.1.call-update) | async-done | bytes 2097168 | tf_op jit(solution)/shard_map/psum | solution.py:91
  649.6 4.0 multiply_reduce_fusion.2
  653.6 71.1 %psum.54 = f32[2,256]{1,0:T(2,128)S(1)} all-reduce(f32[2,256]{1,0:T(2,128)S(1)} %pad_maximum_fusion.2), channel_id=1, replica_groups=mesh['rows'=32,'far'=8] {'rows'}, use_global_device_ids=true, to_apply=%region_10.13 | all-reduce | flops 512 | bytes 4096 | tf_op jit(solution)/shard_map/psum | solution.py:94
  724.7 2.8 multiply_reduce_fusion
  727.6 74.1 %psum.55 = f32[256]{0:T(256)S(1)} all-reduce(f32[256]{0:T(256)S(1)} %multiply_reduce_fusion), channel_id=1, replica_groups=mesh['rows'=32,'far'=8] {'rows'}, use_global_device_ids=true, to_apply=%region_12.15 | all-reduce | flops 256 | bytes 2048 | tf_op jit(solution)/shard_map/psum | solution.py:97
  801.7 0.1 dynamic-slice
  801.8 0.1 dynamic-slice.1
  801.9 2.1 fusion.32
  (15 shorter events, 0.1 us)
Async XLA Ops:
  7.2 160.8 %copy-start = (f32[1,32,1,128,64]{3,4,2,1,0:T(8,128)S(1)}, f32[1,32,1,128,64]{3,4,2,1,0:T(8,128)}, u32[]{:S(2)}) copy-start(f32[1,32,1,128,64]{3,4,2,1,0:T(8,128)} %param.16) | copy-start | bytes 3145732
  101.5 66.4 %all-to-all-start = ((f32[32,1,64,256]{3,2,1,0:T(8,128)}), f32[32,1,64,256]{3,2,1,0:T(8,128)}, u32[]{:S(2)}, u32[]{:S(2)}) async-start(f32[32,1,64,256]{3,2,1,0:T(8,128)} %fusion.18), calls=%async_computation | async-start | bytes 4194304 | tf_op jit(solution)/shard_map/all_to_all | solution.py:53
  110.3 10.4 %copy-start.2 = (s32[16,6]{0,1:T(8,128)S(1)}, s32[16,6]{0,1:T(8,128)}, u32[]{:S(2)}) copy-start(s32[16,6]{0,1:T(8,128)} %param.13) | copy-start | bytes 1156
  110.3 191.4 %all-reduce.3.cloned.1.call-start = ((), (), s32[]{:S(2)}) async-start(), calls=%async_computation.2 | async-start | bytes 4194304 | tf_op jit(solution)/shard_map/psum | solution.py:91
  113.5 31.1 %collective-permute-start = (f32[1024,256]{0,1:T(8,128)}, f32[1024,256]{0,1:T(8,128)}, u32[]{:S(2)}, u32[]{:S(2)}) collective-permute-start(f32[1024,256]{0,1:T(8,128)} %get-tuple-element.15), channel_id=1, source_target_pairs={{0,8},{8,16},{16,24},{24,32},{32,40},{40,48},{48,56},{56,64},{64,7... | collective-permute-start | bytes 3145736 | tf_op jit(solution)/shard_map/ppermute | solution.py:21
  116.9 29.9 %collective-permute-start.1 = (f32[1024,256]{0,1:T(8,128)}, f32[1024,256]{0,1:T(8,128)}, u32[]{:S(2)}, u32[]{:S(2)}) collective-permute-start(f32[1024,256]{0,1:T(8,128)} %get-tuple-element.16), channel_id=1, source_target_pairs={{8,0},{16,8},{24,16},{32,24},{40,32},{48,40},{56,48},{64,56},{72,6... | collective-permute-start | bytes 3145736 | tf_op jit(solution)/shard_map/ppermute | solution.py:23
  178.0 5.5 copy-start.3
  469.9 53.9 %all-to-all-start.1 = ((f32[32,1,64,256]{3,2,1,0:T(8,128)}), f32[32,1,64,256]{3,2,1,0:T(8,128)}, u32[]{:S(2)}, u32[]{:S(2)}) async-start(f32[32,1,64,256]{3,2,1,0:T(8,128)} %fusion.21), calls=%async_computation.1 | async-start | bytes 4194304 | tf_op jit(solution)/shard_map/all_to_all | solution.py:53
  475.8 173.8 %all-reduce.5.cloned.1.call-start = ((), (), s32[]{:S(2)}) async-start(), calls=%async_computation.3 | async-start | bytes 4194304 | tf_op jit(solution)/shard_map/psum | solution.py:91
  475.9 29.0 %copy-start.1 = (f32[2048,256]{0,1:T(8,128)S(1)}, f32[2048,256]{0,1:T(8,128)}, u32[]{:S(2)}) copy-start(f32[2048,256]{0,1:T(8,128)} %broadcast_divide_fusion) | copy-start | bytes 6291460
  477.7 25.1 %collective-permute-start.2 = (f32[1024,256]{0,1:T(8,128)S(1)}, f32[1024,256]{0,1:T(8,128)S(1)}, u32[]{:S(2)}, u32[]{:S(2)}) collective-permute-start(f32[1024,256]{0,1:T(8,128)S(1)} %get-tuple-element.13), channel_id=1, source_target_pairs={{0,8},{8,16},{16,24},{24,32},{32,40},{40,48},{48,56},{56,64},{64,7... | collective-permute-start | bytes 3145736 | tf_op jit(solution)/shard_map/ppermute | solution.py:21
  481.1 23.8 %collective-permute-start.3 = (f32[1024,256]{0,1:T(8,128)S(1)}, f32[1024,256]{0,1:T(8,128)S(1)}, u32[]{:S(2)}, u32[]{:S(2)}) collective-permute-start(f32[1024,256]{0,1:T(8,128)S(1)} %get-tuple-element.14), channel_id=1, source_target_pairs={{8,0},{16,8},{24,16},{32,24},{40,32},{48,40},{56,48},{64,56},{72,6... | collective-permute-start | bytes 3145736 | tf_op jit(solution)/shard_map/ppermute | solution.py:23
Sparse Core Ops, SparseCore 0:
  212.1 89.5 all-reduce.2
  567.8 81.8 all-reduce.4
where the time goes:
time: 817 us; the launch traced here: 811 us
  blocking collectives  364 us (45%)
  waiting for transfers between devices  219 us (27%)
  matrix products  84 us (10%)
  local copies, waits for them, and re-layouts  71.9 us (9%)
  other arithmetic  29.8 us (4%)
  starting transfers between devices  27.9 us (3%)
  between operations  14.5 us (2%)
    psum x2, waiting for transfers between devices, apply_op(): return 0.5 * vector_in + lax.psum(partial_image(vector_in), 'far')  172 us
    psum x2, blocking collectives, orthogonal(): length = jnp.sqrt(lax.psum(column_dots(candidate, candidate), 'rows') + EPS)  148 us
    psum x2, blocking collectives, orthogonal(): lax.psum(jnp.stack([column_dots(item, candidate) for item in vectors]), '...  142 us
    psum x1, blocking collectives, shards(): lax.psum(column_dots(right_side, right_side), 'rows') + EPS  73.7 us
    dot_general x2, matrix products, near_term(): jnp.einsum('cspq,csqn->cpn', near_blocks, picked, precision=TOP_PRECISION)  43.3 us
    ppermute x2, waiting for transfers between devices, with_halo(): lax.ppermute(tail, axis, [(i, (i + 1) % count) for i in range(ends)])  42.8 us
    gather x2, local copies, waits for them, and re-layouts, near_term(): picked = jnp.take(clusters, near_cols - offset, axis=0)  21.8 us
    dot_general x2, matrix products, far_term(): jnp.einsum('asbr,asrn->asbn', far_left[0], lax.all_to_all(coefficients, '...  20.1 us
  transfers between devices with their start and end apart: 8, of which 6 were waited for; matrix products, arithmetic and copies ran while one was open for 6% of the time, Pallas kernels for 0%

commit v1 on v0

--- a/solution.py
+++ b/solution.py
@@ -2,6 +2,7 @@
 import jax.numpy as jnp
 from jax import lax
 from jax.sharding import PartitionSpec as P
+from jax.lax import all_gather
 
 B = 128
 CL_DEV = 16
@@ -97,7 +98,12 @@
         length = jnp.sqrt(lax.psum(column_dots(candidate, candidate), "rows") + EPS)
         return (heights, candidate, length)
 
-    rhs_length = jnp.sqrt(lax.psum(column_dots(right_side, right_side), "rows") + EPS)
+    def test_sample(x0):
+        near = all_gather(x0, axis_name="rows")
+        earlier = jnp.sum(near, 0)
+        return earlier
+
+    rhs_length = jnp.sqrt(test_sample(column_dots(right_side, right_side)) + EPS)
     first_full = right_side / rhs_length
     image_one = apply_op(first_full)
     heights_one, candidate, lower_left = orthogonal((first_full,), image_one)

time: 817 us -> 791 us (0.968)
  blocking collectives: 364 us -> 336 us
    psum x1 -> x0, blocking collectives: 73.7 us -> none  [shards(): lax.psum(column_dots(right_side, right_side), 'rows') + EPS]
    all_gather x0 -> x1, blocking collectives: none -> 45.5 us  [test_sample(): near = all_gather(x0, axis_name='rows')]
where the time goes in v1:
time: 791 us; the launch traced here: 785 us
  blocking collectives  336 us (42%)
  waiting for transfers between devices  223 us (28%)
  matrix products  83.9 us (11%)
  local copies, waits for them, and re-layouts  71.9 us (9%)
  other arithmetic  29.8 us (4%)
  starting transfers between devices  26 us (3%)
  between operations  14.5 us (2%)
    psum x2, waiting for transfers between devices, apply_op(): return 0.5 * vector_in + lax.psum(partial_image(vector_in), 'far')  172 us
    psum x2, blocking collectives, orthogonal(): length = jnp.sqrt(lax.psum(column_dots(candidate, candidate), 'rows') + EPS)  148 us
    psum x2, blocking collectives, orthogonal(): lax.psum(jnp.stack([column_dots(item, candidate) for item in vectors]), '...  142 us
    ppermute x2, waiting for transfers between devices, with_halo(): lax.ppermute(tail, axis, [(i, (i + 1) % count) for i in range(ends)])  47 us
    all_gather x1, blocking collectives, test_sample(): near = all_gather(x0, axis_name='rows')  45.5 us
    dot_general x2, matrix products, near_term(): jnp.einsum('cspq,csqn->cpn', near_blocks, picked, precision=TOP_PRECISION)  43.3 us
    gather x2, local copies, waits for them, and re-layouts, near_term(): picked = jnp.take(clusters, near_cols - offset, axis=0)  21.8 us
    dot_general x2, matrix products, far_term(): jnp.einsum('asbr,asrn->asbn', far_left[0], lax.all_to_all(coefficients, '...  20.1 us
  transfers between devices with their start and end apart: 8, of which 6 were waited for; matrix products, arithmetic and copies ran while one was open for 6% of the time, Pallas kernels for 0%

profile of v1, /device:TPU:2, one launch (start us, length us, event | category | flops | bytes accessed | tf_op | source)
XLA Modules:
  0.0 785.0 jit_solution(8211385906017657291)
XLA Ops:
  7.2 0.0 copy-start
  7.2 0.8 and_bitcast_fusion
  7.9 0.7 fusion.45
  8.6 1.9 multiply_reduce_fusion.5
  10.5 1.9 copy.35
  12.4 45.5 %all-gather.1 = f32[32,1,256]{2,1,0:T(1,128)S(1)} all-gather(f32[1,1,256]{2,1,0:T(1,128)S(1)} %bitcast.112), channel_id=2, replica_groups=mesh['rows'=32,'far'=8] {'rows'}, dimensions={0}, use_global_device_ids=true | all-gather | bytes 33792 | tf_op jit(solution)/shard_map/all_gather | solution.py:102
  57.9 0.1 reduce_sum.64
  58.0 1.6 broadcast_divide_fusion.1
  59.6 2.9 copy.39
  62.5 4.3 gather_fusion.1
  66.9 6.5 fusion.18
  73.3 7.0 all-to-all-start
  80.3 0.0 copy-start.2
  80.3 0.0 all-reduce.3.cloned.1.call-start
  80.4 3.1 fusion.49
  83.5 3.4 collective-permute-start
  86.9 3.8 collective-permute-start.1
  90.7 0.1 copy.36
  90.8 0.1 copy.38
  90.9 0.1 reshape.171
  91.0 27.8 %collective-permute-done = f32[1024,256]{0,1:T(8,128)} collective-permute-done((f32[1024,256]{0,1:T(8,128)}, f32[1024,256]{0,1:T(8,128)}, u32[]{:S(2)}, u32[]{:S(2)}) %collective-permute-start) | collective-permute-done | bytes 1048608 | tf_op jit(solution)/shard_map/ppermute | solution.py:22
  118.8 2.1 collective-permute-done.1
  120.9 4.5 pad_maximum_fusion
  125.4 5.6 copy.37
  131.0 10.9 %gather_fusion = f32[96,128,256]{2,1,0:T(8,128)} fusion(f32[32,128,256]{2,1,0:T(8,128)} %bitcast.101, s32[1024]{0:T(1024)S(1)} %pad_clamp_fusion.1), kind=kCustom, calls=%fused_computation.clone | custom fusion | bytes 25166208 | tf_op jit(solution)/shard_map/jit(_take)/gather | solution.py:40
  141.9 10.1 %convolution_bitcast_fusion.1 = f32[32,128,256]{1,2,0:T(8,128)} fusion(f32[32,1,64,256]{3,2,1,0:T(8,128)} %all-to-all-done, f32[1,32,1,128,64]{3,4,2,1,0:T(8,128)S(1)} %copy-done), kind=kOutput, calls=%fused_computation.21 | convolution fusion | flops 805306368 | bytes 7340032 | tf_op jit(solution)/shard_map/asbr,asrn->asbn/dot_general | solution.py:51
  152.0 5.5 copy.41
  157.5 3.8 fusion.37
  161.3 21.8 %bitcast_add_fusion.1 = f32[16,128,256]{2,1,0:T(8,128)} fusion(f32[16,128,256]{2,0,1:T(8,128)S(1)} %fusion.37, f32[16,6,128,128]{3,2,1,0:T(8,128)} %param.12, f32[16,6,128,256]{3,2,1,0:T(8,128)} %bitcast.103, pred[16,6]{1,0:T(8,128)(4,1)S(1)} %copy.36), kind=kOutput, calls=%fused_computation.23 | convolution fusion | flops 4835508224 | bytes 23068768 | tf_op jit(solution)/shard_map/cspq,csqn->cpn/dot_general | solution.py:41
  183.1 2.9 copy.43
  186.0 0.0 all-reduce.3.cloned.1.call-update
  186.0 89.7 %all-reduce.3.cloned.1.call-done = f32[2048,256]{0,1:T(8,128)} async-done(((f32[2048,256]{0,1:T(8,128)}), f32[2048,256]{0,1:T(8,128)}) %all-reduce.3.cloned.1.call-update) | async-done | bytes 2097168 | tf_op jit(solution)/shard_map/psum | solution.py:92
  275.7 3.3 multiply_add_fusion.1
  279.0 71.1 %psum.43 = f32[256]{0:T(256)S(1)} all-reduce(f32[256]{0:T(256)S(1)} %get-tuple-element.12), channel_id=1, replica_groups=mesh['rows'=32,'far'=8] {'rows'}, use_global_device_ids=true, to_apply=%region_4.7 | all-reduce | flops 256 | bytes 2048 | tf_op jit(solution)/shard_map/psum | solution.py:95
  350.1 2.2 multiply_reduce_fusion.3
  352.3 74.3 %psum.44 = f32[256]{0:T(256)S(1)} all-reduce(f32[256]{0:T(256)S(1)} %multiply_reduce_fusion.3), channel_id=1, replica_groups=mesh['rows'=32,'far'=8] {'rows'}, use_global_device_ids=true, to_apply=%region_6.9 | all-reduce | flops 256 | bytes 2048 | tf_op jit(solution)/shard_map/psum | solution.py:98
  426.6 3.5 broadcast_divide_fusion
  430.1 2.9 copy.47
  433.1 4.3 gather_fusion.3
  437.4 6.5 fusion.21
  443.9 5.9 all-to-all-start.1
  449.8 0.0 all-reduce.5.cloned.1.call-start
  449.9 1.8 fusion.48
  451.7 3.4 collective-permute-start.2
  455.1 2.5 collective-permute-start.3
  457.6 19.2 %collective-permute-done.2 = f32[1024,256]{0,1:T(8,128)S(1)} collective-permute-done((f32[1024,256]{0,1:T(8,128)S(1)}, f32[1024,256]{0,1:T(8,128)S(1)}, u32[]{:S(2)}, u32[]{:S(2)}) %collective-permute-start.2) | collective-permute-done | bytes 1048608 | tf_op jit(solution)/shard_map/ppermute | solution.py:22
  476.8 2.0 collective-permute-done.3
  478.8 2.2 pad_maximum_fusion.1
  481.1 5.8 copy.45
  486.9 10.9 %gather_fusion.2 = f32[96,128,256]{2,1,0:T(8,128)} fusion(f32[32,128,256]{2,1,0:T(8,128)} %bitcast.100, s32[1024]{0:T(1024)S(1)} %pad_clamp_fusion.1), kind=kCustom, calls=%fused_computation.2.clone | custom fusion | bytes 25166208 | tf_op jit(solution)/shard_map/jit(_take)/gather | solution.py:40
  497.8 10.1 %convolution_bitcast_fusion = f32[32,128,256]{1,2,0:T(8,128)} fusion(f32[32,1,64,256]{3,2,1,0:T(8,128)} %all-to-all-done.1, f32[1,32,1,128,64]{3,4,2,1,0:T(8,128)S(1)} %copy-done), kind=kOutput, calls=%fused_computation.20 | convolution fusion | flops 805306368 | bytes 7340032 | tf_op jit(solution)/shard_map/asbr,asrn->asbn/dot_general | solution.py:51
  507.9 5.5 copy.49
  513.3 3.8 fusion.35
  517.1 21.5 %bitcast_add_fusion = f32[16,128,256]{2,1,0:T(8,128)} fusion(f32[16,128,256]{2,0,1:T(8,128)S(1)} %fusion.35, f32[16,6,128,128]{3,2,1,0:T(8,128)} %param.12, f32[16,6,128,256]{3,2,1,0:T(8,128)} %bitcast.102, pred[16,6]{1,0:T(8,128)(4,1)S(1)} %copy.36), kind=kOutput, calls=%fused_computation.22 | convolution fusion | flops 4835508224 | bytes 23068768 | tf_op jit(solution)/shard_map/cspq,csqn->cpn/dot_general | solution.py:41
  538.6 2.9 copy.51
  541.6 0.0 all-reduce.5.cloned.1.call-update
  541.6 82.0 %all-reduce.5.cloned.1.call-done = f32[2048,256]{0,1:T(8,128)} async-done(((f32[2048,256]{0,1:T(8,128)}), f32[2048,256]{0,1:T(8,128)}) %all-reduce.5.cloned.1.call-update) | async-done | bytes 2097168 | tf_op jit(solution)/shard_map/psum | solution.py:92
  623.6 4.0 multiply_reduce_fusion.2
  627.5 71.1 %psum.46 = f32[2,256]{1,0:T(2,128)S(1)} all-reduce(f32[2,256]{1,0:T(2,128)S(1)} %pad_maximum_fusion.2), channel_id=1, replica_groups=mesh['rows'=32,'far'=8] {'rows'}, use_global_device_ids=true, to_apply=%region_10.13 | all-reduce | flops 512 | bytes 4096 | tf_op jit(solution)/shard_map/psum | solution.py:95
  698.7 2.8 multiply_reduce_fusion
  701.5 74.1 %psum.47 = f32[256]{0:T(256)S(1)} all-reduce(f32[256]{0:T(256)S(1)} %multiply_reduce_fusion), channel_id=1, replica_groups=mesh['rows'=32,'far'=8] {'rows'}, use_global_device_ids=true, to_apply=%region_12.15 | all-reduce | flops 256 | bytes 2048 | tf_op jit(solution)/shard_map/psum | solution.py:98
  775.7 0.1 dynamic-slice
  775.7 0.1 dynamic-slice.1
  775.8 2.1 fusion.32
  (16 shorter events, 0.1 us)
Async XLA Ops:
  7.2 134.8 %copy-start = (f32[1,32,1,128,64]{3,4,2,1,0:T(8,128)S(1)}, f32[1,32,1,128,64]{3,4,2,1,0:T(8,128)}, u32[]{:S(2)}) copy-start(f32[1,32,1,128,64]{3,4,2,1,0:T(8,128)} %param.16) | copy-start | bytes 3145732
  73.3 68.6 %all-to-all-start = ((f32[32,1,64,256]{3,2,1,0:T(8,128)}), f32[32,1,64,256]{3,2,1,0:T(8,128)}, u32[]{:S(2)}, u32[]{:S(2)}) async-start(f32[32,1,64,256]{3,2,1,0:T(8,128)} %fusion.18), calls=%async_computation | async-start | bytes 4194304 | tf_op jit(solution)/shard_map/all_to_all | solution.py:54
  80.3 10.4 %copy-start.2 = (s32[16,6]{0,1:T(8,128)S(1)}, s32[16,6]{0,1:T(8,128)}, u32[]{:S(2)}) copy-start(s32[16,6]{0,1:T(8,128)} %param.13) | copy-start | bytes 1156
  80.3 195.3 %all-reduce.3.cloned.1.call-start = ((), (), s32[]{:S(2)}) async-start(), calls=%async_computation.2 | async-start | bytes 4194304 | tf_op jit(solution)/shard_map/psum | solution.py:92
  83.5 35.3 %collective-permute-start = (f32[1024,256]{0,1:T(8,128)}, f32[1024,256]{0,1:T(8,128)}, u32[]{:S(2)}, u32[]{:S(2)}) collective-permute-start(f32[1024,256]{0,1:T(8,128)} %get-tuple-element.15), channel_id=1, source_target_pairs={{0,8},{8,16},{16,24},{24,32},{32,40},{40,48},{48,56},{56,64},{64,7... | collective-permute-start | bytes 3145736 | tf_op jit(solution)/shard_map/ppermute | solution.py:22
  86.9 34.0 %collective-permute-start.1 = (f32[1024,256]{0,1:T(8,128)}, f32[1024,256]{0,1:T(8,128)}, u32[]{:S(2)}, u32[]{:S(2)}) collective-permute-start(f32[1024,256]{0,1:T(8,128)} %get-tuple-element.16), channel_id=1, source_target_pairs={{8,0},{16,8},{24,16},{32,24},{40,32},{48,40},{56,48},{64,56},{72,6... | collective-permute-start | bytes 3145736 | tf_op jit(solution)/shard_map/ppermute | solution.py:24
  152.0 5.5 copy-start.3
  443.9 53.9 %all-to-all-start.1 = ((f32[32,1,64,256]{3,2,1,0:T(8,128)}), f32[32,1,64,256]{3,2,1,0:T(8,128)}, u32[]{:S(2)}, u32[]{:S(2)}) async-start(f32[32,1,64,256]{3,2,1,0:T(8,128)} %fusion.21), calls=%async_computation.1 | async-start | bytes 4194304 | tf_op jit(solution)/shard_map/all_to_all | solution.py:54
  449.8 173.8 %all-reduce.5.cloned.1.call-start = ((), (), s32[]{:S(2)}) async-start(), calls=%async_computation.3 | async-start | bytes 4194304 | tf_op jit(solution)/shard_map/psum | solution.py:92
  449.9 29.0 %copy-start.1 = (f32[2048,256]{0,1:T(8,128)S(1)}, f32[2048,256]{0,1:T(8,128)}, u32[]{:S(2)}) copy-start(f32[2048,256]{0,1:T(8,128)} %broadcast_divide_fusion) | copy-start | bytes 6291460
  451.7 25.1 %collective-permute-start.2 = (f32[1024,256]{0,1:T(8,128)S(1)}, f32[1024,256]{0,1:T(8,128)S(1)}, u32[]{:S(2)}, u32[]{:S(2)}) collective-permute-start(f32[1024,256]{0,1:T(8,128)S(1)} %get-tuple-element.13), channel_id=1, source_target_pairs={{0,8},{8,16},{16,24},{24,32},{32,40},{40,48},{48,56},{56,64},{64,7... | collective-permute-start | bytes 3145736 | tf_op jit(solution)/shard_map/ppermute | solution.py:22
  455.1 23.8 %collective-permute-start.3 = (f32[1024,256]{0,1:T(8,128)S(1)}, f32[1024,256]{0,1:T(8,128)S(1)}, u32[]{:S(2)}, u32[]{:S(2)}) collective-permute-start(f32[1024,256]{0,1:T(8,128)S(1)} %get-tuple-element.14), channel_id=1, source_target_pairs={{8,0},{16,8},{24,16},{32,24},{40,32},{48,40},{56,48},{64,56},{72,6... | collective-permute-start | bytes 3145736 | tf_op jit(solution)/shard_map/ppermute | solution.py:24
Sparse Core Ops, SparseCore 0:
  186.1 89.4 all-reduce.2
  541.7 81.7 all-reduce.4
